TPU v7x, 256 devices: a whole 4x4x8 slice. The times are simulated.
256 devices in a mesh: blk: 64 (over y, x_lo, z), rep: 4 (over x_hi, core).
Axes of the slice: x: 4 (x_hi: 2, x_lo: 2; x = x_hi * 2 + x_lo), y: 4, z: 8, core: 2. Of those that a mesh axis runs over, the one named last changes fastest.
Arguments:
- tile_vals: bfloat16 [64, 8, 20, 128, 128], P('blk', 'rep'), may hold values from -4 to 4
- tile_coords: int32 [64, 8, 20, 2], P('blk', 'rep'), may hold values from 0 to 3
- tile_live: int32 [64, 8, 20], P('blk', 'rep'), may hold values from 0 to 1, as said below
- features: bfloat16 [32768, 256], P('blk'), may hold values from -6 to 6
- degree: int32 [32768], P(('blk', 'rep')), may hold values from 512 to 8192
- w_self: bfloat16 [256, 256], replicated, may hold values from -0.375 to 0.375
- w_neigh: bfloat16 [256, 256], replicated, may hold values from -0.375 to 0.375
- cotangent: bfloat16 [32768, 256], P(('blk', 'rep')), may hold values from -6 to 6
Outputs:
- hidden: bfloat16 [32768, 256], P(('blk', 'rep'))
- grad_features: bfloat16 [32768, 256], P(('blk', 'rep'))
- grad_self: float32 [256, 256], replicated
- grad_neigh: float32 [256, 256], replicated
Inputs may be any that keep to these rules, and one draw needn't show every extreme that they name: `tile_coords`: entry 0 names a tile row block of the row partition, entry 1 a tile column block of the column partition; tiles with equal coordinates add. `tile_live`: 1 marks a present tile, 0 a padding tile; the share of present tiles differs between row partitions.
All inputs are finite; a program needn't handle non-finite values.
Results may differ from a plain program's by a relative error of at most 0.012.
Values may be sent and summed in bfloat16 or wider, within the bound.
A program may use at most 64 MiB of HBM per device.

v0:
```python
import math

import jax
import jax.numpy as jnp
from jax import lax
from jax.sharding import PartitionSpec as P


def from_behind(value, axis, steps):
    count = lax.axis_size(axis)
    pairs = [(source, (source + steps) % count) for source in range(count)]
    return lax.ppermute(value, axis, pairs)


def on_device(tile_vals, tile_coords, tile_live, features, degree, w_self, w_neigh, cotangent):
    part_total = lax.axis_size("blk")
    rep_count = lax.axis_size("rep")
    rep_id = lax.axis_index("rep")
    step_count = tile_vals.shape[1]
    offset_count = step_count * rep_count
    half_span = offset_count // 2
    tile_size = tile_vals.shape[3]
    row_count, feature_dim = features.shape
    block_count = row_count // tile_size
    share_rows = row_count // rep_count
    live_flags = tile_live[0].astype(jnp.bfloat16)
    masked = tile_vals[0] * live_flags[:, :, None, None]
    row_ids = tile_coords[0, :, :, 0]
    col_ids = tile_coords[0, :, :, 1]

    def forward_term(slot_idx, panel_now):
        blocked = panel_now.reshape(block_count, tile_size, feature_dim)
        sources = blocked[col_ids[slot_idx]]
        products = jnp.einsum(
            "krc,kcd->krd", masked[slot_idx], sources, preferred_element_type=jnp.float32
        )
        placed = (
            jnp.zeros((block_count, tile_size, feature_dim), jnp.float32)
            .at[row_ids[slot_idx]]
            .add(products)
        )
        return placed.reshape(row_count, feature_dim)

    panel_now = from_behind(features, "blk", half_span)
    slots = [features for slot_idx in range(step_count)]
    for offset_idx in range(offset_count):
        slot_idx = offset_idx % step_count
        slots[slot_idx] = jnp.where(rep_id == offset_idx // step_count, panel_now, slots[slot_idx])
        if offset_idx + 1 < offset_count:
            panel_now = from_behind(panel_now, "blk", -1)
    summed = forward_term(0, slots[0])
    slot_idx = 1
    summed = summed + forward_term(slot_idx, slots[slot_idx])
    shared = lax.psum_scatter(summed, "rep", scatter_dimension=0, tiled=True)
    root_deg = jnp.sqrt(degree.astype(jnp.float32))[:, None]
    aggregate = (shared / root_deg).astype(jnp.bfloat16)
    own_rows = lax.dynamic_slice_in_dim(features, rep_id * share_rows, share_rows, 0)
    preact = jnp.dot(own_rows, w_self, preferred_element_type=jnp.float32) + jnp.dot(
        aggregate, w_neigh, preferred_element_type=jnp.float32
    )
    sigmoid_pre = jax.nn.sigmoid(preact)
    hidden = (preact * sigmoid_pre).astype(jnp.bfloat16)
    silu_slope = sigmoid_pre * (1.0 + preact * (1.0 - sigmoid_pre))
    grad_pre = (cotangent.astype(jnp.float32) * silu_slope).astype(jnp.bfloat16)
    local_self = jnp.einsum("nd,ne->de", own_rows, grad_pre, preferred_element_type=jnp.float32)
    local_neigh = jnp.einsum("nd,ne->de", aggregate, grad_pre, preferred_element_type=jnp.float32)
    total_self, total_neigh = lax.psum((local_self, local_neigh), ("blk", "rep"))
    grad_scale = 1.0 / math.sqrt(row_count * part_total)
    back_proj = (
        jnp.einsum("ne,de->nd", grad_pre, w_neigh, preferred_element_type=jnp.float32) / root_deg
    ).astype(jnp.bfloat16)
    full_back = lax.all_gather(back_proj, "rep", axis=0, tiled=True)
    back_blocks = full_back.reshape(block_count, tile_size, feature_dim)

    def backward_term(slot_idx):
        sources = back_blocks[row_ids[slot_idx]]
        products = jnp.einsum(
            "krc,krd->kcd", masked[slot_idx], sources, preferred_element_type=jnp.float32
        )
        placed = (
            jnp.zeros((block_count, tile_size, feature_dim), jnp.float32)
            .at[col_ids[slot_idx]]
            .add(products)
        )
        return placed.reshape(row_count, feature_dim)

    terms = [backward_term(slot_idx) for slot_idx in range(step_count)]
    carried = jnp.zeros((row_count, feature_dim), jnp.float32)
    for offset_idx in range(offset_count):
        mine = rep_id == offset_idx // step_count
        carried = carried + jnp.where(mine, terms[offset_idx % step_count], 0.0)
        if offset_idx + 1 < offset_count:
            carried = from_behind(carried.astype(jnp.bfloat16), "blk", -1).astype(carried.dtype)
    carried = from_behind(carried.astype(jnp.bfloat16), "blk", offset_count - 1 - half_span).astype(
        carried.dtype
    )
    neighbour = lax.psum_scatter(
        carried.astype(jnp.bfloat16), "rep", scatter_dimension=0, tiled=True
    ).astype(jnp.float32)
    own_term = jnp.einsum("ne,de->nd", grad_pre, w_self, preferred_element_type=jnp.float32)
    grad_features = (own_term + neighbour).astype(jnp.bfloat16)
    return (hidden, grad_features, total_self * grad_scale, total_neigh * grad_scale)


def solution(mesh):
    return jax.shard_map(
        on_device,
        mesh=mesh,
        in_specs=(
            P("blk", "rep", None, None, None),
            P("blk", "rep", None, None),
            P("blk", "rep", None),
            P("blk", None),
            P(("blk", "rep")),
            P(),
            P(),
            P(("blk", "rep"), None),
        ),
        out_specs=(P(("blk", "rep"), None), P(("blk", "rep"), None), P(), P()),
        check_vma=False,
    )
```

profile of v0, /device:TPU:1, one launch (start us, length us, event | category | flops | bytes accessed | tf_op | source)
XLA Modules:
  0.0 551.6 jit_solution(10930375766060758941)
XLA Ops:
  7.2 7.8 %collective-permute-start = (bf16[512,256]{1,0:T(8,128)(2,1)}, bf16[512,256]{1,0:T(8,128)(2,1)S(1)}, u32[]{:S(2)}, u32[]{:S(2)}) collective-permute-start(bf16[512,256]{1,0:T(8,128)(2,1)} %param.11), channel_id=1, source_target_pairs={{0,16},{4,20},{8,24},{12,28},{16,32},{20,36},{24,40},{28,44},{32,4... | collective-permute-start | bytes 786440 | tf_op jit(solution)/shard_map/ppermute | solution.py:12
  15.0 10.5 %collective-permute-done = bf16[512,256]{1,0:T(8,128)(2,1)S(1)} collective-permute-done((bf16[512,256]{1,0:T(8,128)(2,1)}, bf16[512,256]{1,0:T(8,128)(2,1)S(1)}, u32[]{:S(2)}, u32[]{:S(2)}) %collective-permute-start) | collective-permute-done | bytes 262176 | tf_op jit(solution)/shard_map/ppermute | solution.py:12
  25.5 5.7 %collective-permute-start.1 = (bf16[512,256]{1,0:T(8,128)(2,1)S(1)}, bf16[512,256]{1,0:T(8,128)(2,1)S(1)}, u32[]{:S(2)}, u32[]{:S(2)}) collective-permute-start(bf16[512,256]{1,0:T(8,128)(2,1)S(1)} %collective-permute-done), channel_id=1, source_target_pairs={{0,252},{4,0},{8,4},{12,8},{16,12},{20,16},{24,20},{28,24},{32,28}... | collective-permute-start | bytes 786440 | tf_op jit(solution)/shard_map/ppermute | solution.py:12
  36.3 5.9 %collective-permute-start.2 = (bf16[512,256]{1,0:T(8,128)(2,1)S(1)}, bf16[512,256]{1,0:T(8,128)(2,1)S(1)}, u32[]{:S(2)}, u32[]{:S(2)}) collective-permute-start(bf16[512,256]{1,0:T(8,128)(2,1)S(1)} %collective-permute-done.1), channel_id=1, source_target_pairs={{0,252},{4,0},{8,4},{12,8},{16,12},{20,16},{24,20},{28,24},{32,28}... | collective-permute-start | bytes 786440 | tf_op jit(solution)/shard_map/ppermute | solution.py:12
  46.0 6.4 %collective-permute-start.3 = (bf16[512,256]{1,0:T(8,128)(2,1)S(1)}, bf16[512,256]{1,0:T(8,128)(2,1)S(1)}, u32[]{:S(2)}, u32[]{:S(2)}) collective-permute-start(bf16[512,256]{1,0:T(8,128)(2,1)S(1)} %collective-permute-done.2), channel_id=1, source_target_pairs={{0,252},{4,0},{8,4},{12,8},{16,12},{20,16},{24,20},{28,24},{32,28}... | collective-permute-start | bytes 786440 | tf_op jit(solution)/shard_map/ppermute | solution.py:12
  55.8 6.1 %collective-permute-start.4 = (bf16[512,256]{1,0:T(8,128)(2,1)S(1)}, bf16[512,256]{1,0:T(8,128)(2,1)S(1)}, u32[]{:S(2)}, u32[]{:S(2)}) collective-permute-start(bf16[512,256]{1,0:T(8,128)(2,1)S(1)} %collective-permute-done.3), channel_id=1, source_target_pairs={{0,252},{4,0},{8,4},{12,8},{16,12},{20,16},{24,20},{28,24},{32,28}... | collective-permute-start | bytes 786440 | tf_op jit(solution)/shard_map/ppermute | solution.py:12
  65.2 6.1 %collective-permute-start.5 = (bf16[512,256]{1,0:T(8,128)(2,1)S(1)}, bf16[512,256]{1,0:T(8,128)(2,1)S(1)}, u32[]{:S(2)}, u32[]{:S(2)}) collective-permute-start(bf16[512,256]{1,0:T(8,128)(2,1)S(1)} %collective-permute-done.4), channel_id=1, source_target_pairs={{0,252},{4,0},{8,4},{12,8},{16,12},{20,16},{24,20},{28,24},{32,28}... | collective-permute-start | bytes 786440 | tf_op jit(solution)/shard_map/ppermute | solution.py:12
  74.6 6.1 %collective-permute-start.6 = (bf16[512,256]{1,0:T(8,128)(2,1)S(1)}, bf16[512,256]{1,0:T(8,128)(2,1)S(1)}, u32[]{:S(2)}, u32[]{:S(2)}) collective-permute-start(bf16[512,256]{1,0:T(8,128)(2,1)S(1)} %collective-permute-done.5), channel_id=1, source_target_pairs={{0,252},{4,0},{8,4},{12,8},{16,12},{20,16},{24,20},{28,24},{32,28}... | collective-permute-start | bytes 786440 | tf_op jit(solution)/shard_map/ppermute | solution.py:12
  84.1 6.1 %collective-permute-start.7 = (bf16[512,256]{1,0:T(8,128)(2,1)S(1)}, bf16[512,256]{1,0:T(8,128)(2,1)S(1)}, u32[]{:S(2)}, u32[]{:S(2)}) collective-permute-start(bf16[512,256]{1,0:T(8,128)(2,1)S(1)} %collective-permute-done.6), channel_id=1, source_target_pairs={{0,252},{4,0},{8,4},{12,8},{16,12},{20,16},{24,20},{28,24},{32,28}... | collective-permute-start | bytes 786440 | tf_op jit(solution)/shard_map/ppermute | solution.py:12
  99.1 5.9 %scatter_fusion.1 = f32[4,128,256]{2,1,0:T(8,128)S(1)} fusion(f32[4,128,256]{2,1,0:T(8,128)S(1)} %broadcast.93.clone.1, s32[20]{0:T(128)S(1)} %copy-done.8, f32[20,128,256]{2,1,0:T(8,128)} %fusion.4), kind=kCustom, calls=%fused_computation.5 | custom fusion | flops 655360 | bytes 7864400 | tf_op jit(solution)/shard_map/scatter-add | solution.py:40
  105.1 5.9 %scatter_fusion = f32[4,128,256]{2,1,0:T(8,128)S(1)} fusion(f32[4,128,256]{2,1,0:T(8,128)S(1)} %broadcast.93.clone, s32[20]{0:T(128)S(1)} %copy-done.7, f32[20,128,256]{2,1,0:T(8,128)} %fusion.2), kind=kCustom, calls=%fused_computation.4 | custom fusion | flops 655360 | bytes 7864400 | tf_op jit(solution)/shard_map/scatter-add | solution.py:40
  112.1 40.7 %reduce-scatter.3.cloned.1.call-done = f32[128,256]{1,0:T(8,128)} async-done(((f32[512,256]{1,0:T(8,128)}), f32[128,256]{1,0:T(8,128)}) %reduce-scatter.3.cloned.1.call-update) | async-done | bytes 131088 | tf_op jit(solution)/shard_map/reduce_scatter | solution.py:54
  154.9 8.1 %all_gather.3 = bf16[512,256]{1,0:T(8,128)(2,1)S(1)} all-gather(bf16[128,256]{1,0:T(8,128)(2,1)S(1)} %fusion), channel_id=1, replica_groups=mesh['blk'=64,'rep'=4] {'rep'}, dimensions={0}, use_global_device_ids=true | all-gather | bytes 327680 | tf_op jit(solution)/shard_map/all_gather | solution.py:72
  168.5 5.9 %scatter_fusion.2 = f32[4,128,256]{2,1,0:T(8,128)S(1)} fusion(f32[4,128,256]{2,1,0:T(8,128)S(1)} %broadcast.93.clone.3, s32[20]{0:T(128)S(1)} %get-tuple-element.18, f32[20,128,256]{2,1,0:T(8,128)} %fusion.1), kind=kCustom, calls=%fused_computation.6 | custom fusion | flops 655360 | bytes 7864400 | tf_op jit(solution)/shard_map/scatter-add | solution.py:83
  179.8 5.9 %scatter_fusion.3 = f32[4,128,256]{2,1,0:T(8,128)S(1)} fusion(f32[4,128,256]{2,1,0:T(8,128)S(1)} %broadcast.93.clone.2, s32[20]{0:T(128)S(1)} %get-tuple-element.17, f32[20,128,256]{2,1,0:T(8,128)} %fusion.3), kind=kCustom, calls=%fused_computation.7 | custom fusion | flops 655360 | bytes 7864400 | tf_op jit(solution)/shard_map/scatter-add | solution.py:83
  186.0 5.8 %collective-permute-start.9 = (bf16[512,256]{1,0:T(8,128)(2,1)S(1)}, bf16[512,256]{1,0:T(8,128)(2,1)S(1)}, u32[]{:S(2)}, u32[]{:S(2)}) collective-permute-start(bf16[512,256]{1,0:T(8,128)(2,1)S(1)} %fusion.11), channel_id=1, source_target_pairs={{0,252},{4,0},{8,4},{12,8},{16,12},{20,16},{24,20},{28,24},{32,28}... | collective-permute-start | bytes 786440 | tf_op jit(solution)/shard_map/ppermute | solution.py:12
  196.5 6.5 %collective-permute-start.10 = (bf16[512,256]{1,0:T(8,128)(2,1)S(1)}, bf16[512,256]{1,0:T(8,128)(2,1)S(1)}, u32[]{:S(2)}, u32[]{:S(2)}) collective-permute-start(bf16[512,256]{1,0:T(8,128)(2,1)S(1)} %fusion.10), channel_id=1, source_target_pairs={{0,252},{4,0},{8,4},{12,8},{16,12},{20,16},{24,20},{28,24},{32,28}... | collective-permute-start | bytes 786440 | tf_op jit(solution)/shard_map/ppermute | solution.py:12
  206.9 6.5 %collective-permute-start.11 = (bf16[512,256]{1,0:T(8,128)(2,1)S(1)}, bf16[512,256]{1,0:T(8,128)(2,1)S(1)}, u32[]{:S(2)}, u32[]{:S(2)}) collective-permute-start(bf16[512,256]{1,0:T(8,128)(2,1)S(1)} %fusion.9), channel_id=1, source_target_pairs={{0,252},{4,0},{8,4},{12,8},{16,12},{20,16},{24,20},{28,24},{32,28}... | collective-permute-start | bytes 786440 | tf_op jit(solution)/shard_map/ppermute | solution.py:12
  216.8 6.2 %collective-permute-start.12 = (bf16[512,256]{1,0:T(8,128)(2,1)S(1)}, bf16[512,256]{1,0:T(8,128)(2,1)S(1)}, u32[]{:S(2)}, u32[]{:S(2)}) collective-permute-start(bf16[512,256]{1,0:T(8,128)(2,1)S(1)} %fusion.8), channel_id=1, source_target_pairs={{0,252},{4,0},{8,4},{12,8},{16,12},{20,16},{24,20},{28,24},{32,28}... | collective-permute-start | bytes 786440 | tf_op jit(solution)/shard_map/ppermute | solution.py:12
  226.3 6.2 %collective-permute-start.13 = (bf16[512,256]{1,0:T(8,128)(2,1)S(1)}, bf16[512,256]{1,0:T(8,128)(2,1)S(1)}, u32[]{:S(2)}, u32[]{:S(2)}) collective-permute-start(bf16[512,256]{1,0:T(8,128)(2,1)S(1)} %fusion.7), channel_id=1, source_target_pairs={{0,252},{4,0},{8,4},{12,8},{16,12},{20,16},{24,20},{28,24},{32,28}... | collective-permute-start | bytes 786440 | tf_op jit(solution)/shard_map/ppermute | solution.py:12
  235.9 6.2 %collective-permute-start.14 = (bf16[512,256]{1,0:T(8,128)(2,1)S(1)}, bf16[512,256]{1,0:T(8,128)(2,1)S(1)}, u32[]{:S(2)}, u32[]{:S(2)}) collective-permute-start(bf16[512,256]{1,0:T(8,128)(2,1)S(1)} %fusion.6), channel_id=1, source_target_pairs={{0,252},{4,0},{8,4},{12,8},{16,12},{20,16},{24,20},{28,24},{32,28}... | collective-permute-start | bytes 786440 | tf_op jit(solution)/shard_map/ppermute | solution.py:12
  246.6 10.5 %collective-permute-done.15 = bf16[512,256]{1,0:T(8,128)(2,1)S(1)} collective-permute-done((bf16[512,256]{1,0:T(8,128)(2,1)S(1)}, bf16[512,256]{1,0:T(8,128)(2,1)S(1)}, u32[]{:S(2)}, u32[]{:S(2)}) %collective-permute-start.15) | collective-permute-done | bytes 262176 | tf_op jit(solution)/shard_map/ppermute | solution.py:12
  258.0 250.7 %all-reduce.3.cloned.1.call-done = (f32[256,256]{1,0:T(8,128)}, f32[256,256]{1,0:T(8,128)}) async-done(((f32[256,256]{1,0:T(8,128)}, f32[256,256]{1,0:T(8,128)}), (f32[256,256]{1,0:T(8,128)}, f32[256,256]{1,0:T(8,128)})) %all-reduce.3.cloned.1.call-update) | async-done | bytes 524304 | tf_op jit(solution)/shard_map/psum | solution.py:67
  512.0 31.6 %reduce-scatter.5.cloned.1.call-done = bf16[128,256]{1,0:T(8,128)(2,1)} async-done(((bf16[512,256]{1,0:T(8,128)(2,1)}), bf16[128,256]{1,0:T(8,128)(2,1)}) %reduce-scatter.5.cloned.1.call-update) | async-done | bytes 65552 | tf_op jit(solution)/shard_map/reduce_scatter | solution.py:97
  (89 shorter events, 74.1 us)
Async XLA Ops:
  7.2 145.7 %copy-start = (bf16[256,256]{1,0:T(8,128)(2,1)S(1)}, bf16[256,256]{1,0:T(8,128)(2,1)}, u32[]{:S(2)}) copy-start(bf16[256,256]{1,0:T(8,128)(2,1)} %param.14) | copy-start | bytes 393220
  7.2 145.7 %reduce-scatter.3.cloned.1.call-start = ((), (), s32[]{:S(2)}) async-start(), calls=%async_computation.2 | async-start | bytes 655360 | tf_op jit(solution)/shard_map/reduce_scatter | solution.py:54
  7.2 18.3 %collective-permute-start = (bf16[512,256]{1,0:T(8,128)(2,1)}, bf16[512,256]{1,0:T(8,128)(2,1)S(1)}, u32[]{:S(2)}, u32[]{:S(2)}) collective-permute-start(bf16[512,256]{1,0:T(8,128)(2,1)} %param.11), channel_id=1, source_target_pairs={{0,16},{4,20},{8,24},{12,28},{16,32},{20,36},{24,40},{28,44},{32,4... | collective-permute-start | bytes 786440 | tf_op jit(solution)/shard_map/ppermute | solution.py:12
  25.5 10.8 %collective-permute-start.1 = (bf16[512,256]{1,0:T(8,128)(2,1)S(1)}, bf16[512,256]{1,0:T(8,128)(2,1)S(1)}, u32[]{:S(2)}, u32[]{:S(2)}) collective-permute-start(bf16[512,256]{1,0:T(8,128)(2,1)S(1)} %collective-permute-done), channel_id=1, source_target_pairs={{0,252},{4,0},{8,4},{12,8},{16,12},{20,16},{24,20},{28,24},{32,28}... | collective-permute-start | bytes 786440 | tf_op jit(solution)/shard_map/ppermute | solution.py:12
  36.3 9.7 %collective-permute-start.2 = (bf16[512,256]{1,0:T(8,128)(2,1)S(1)}, bf16[512,256]{1,0:T(8,128)(2,1)S(1)}, u32[]{:S(2)}, u32[]{:S(2)}) collective-permute-start(bf16[512,256]{1,0:T(8,128)(2,1)S(1)} %collective-permute-done.1), channel_id=1, source_target_pairs={{0,252},{4,0},{8,4},{12,8},{16,12},{20,16},{24,20},{28,24},{32,28}... | collective-permute-start | bytes 786440 | tf_op jit(solution)/shard_map/ppermute | solution.py:12
  46.0 9.7 %collective-permute-start.3 = (bf16[512,256]{1,0:T(8,128)(2,1)S(1)}, bf16[512,256]{1,0:T(8,128)(2,1)S(1)}, u32[]{:S(2)}, u32[]{:S(2)}) collective-permute-start(bf16[512,256]{1,0:T(8,128)(2,1)S(1)} %collective-permute-done.2), channel_id=1, source_target_pairs={{0,252},{4,0},{8,4},{12,8},{16,12},{20,16},{24,20},{28,24},{32,28}... | collective-permute-start | bytes 786440 | tf_op jit(solution)/shard_map/ppermute | solution.py:12
  55.8 9.4 %collective-permute-start.4 = (bf16[512,256]{1,0:T(8,128)(2,1)S(1)}, bf16[512,256]{1,0:T(8,128)(2,1)S(1)}, u32[]{:S(2)}, u32[]{:S(2)}) collective-permute-start(bf16[512,256]{1,0:T(8,128)(2,1)S(1)} %collective-permute-done.3), channel_id=1, source_target_pairs={{0,252},{4,0},{8,4},{12,8},{16,12},{20,16},{24,20},{28,24},{32,28}... | collective-permute-start | bytes 786440 | tf_op jit(solution)/shard_map/ppermute | solution.py:12
  65.2 9.4 %collective-permute-start.5 = (bf16[512,256]{1,0:T(8,128)(2,1)S(1)}, bf16[512,256]{1,0:T(8,128)(2,1)S(1)}, u32[]{:S(2)}, u32[]{:S(2)}) collective-permute-start(bf16[512,256]{1,0:T(8,128)(2,1)S(1)} %collective-permute-done.4), channel_id=1, source_target_pairs={{0,252},{4,0},{8,4},{12,8},{16,12},{20,16},{24,20},{28,24},{32,28}... | collective-permute-start | bytes 786440 | tf_op jit(solution)/shard_map/ppermute | solution.py:12
  74.6 9.4 %collective-permute-start.6 = (bf16[512,256]{1,0:T(8,128)(2,1)S(1)}, bf16[512,256]{1,0:T(8,128)(2,1)S(1)}, u32[]{:S(2)}, u32[]{:S(2)}) collective-permute-start(bf16[512,256]{1,0:T(8,128)(2,1)S(1)} %collective-permute-done.5), channel_id=1, source_target_pairs={{0,252},{4,0},{8,4},{12,8},{16,12},{20,16},{24,20},{28,24},{32,28}... | collective-permute-start | bytes 786440 | tf_op jit(solution)/shard_map/ppermute | solution.py:12
  84.1 9.5 %collective-permute-start.7 = (bf16[512,256]{1,0:T(8,128)(2,1)S(1)}, bf16[512,256]{1,0:T(8,128)(2,1)S(1)}, u32[]{:S(2)}, u32[]{:S(2)}) collective-permute-start(bf16[512,256]{1,0:T(8,128)(2,1)S(1)} %collective-permute-done.6), channel_id=1, source_target_pairs={{0,252},{4,0},{8,4},{12,8},{16,12},{20,16},{24,20},{28,24},{32,28}... | collective-permute-start | bytes 786440 | tf_op jit(solution)/shard_map/ppermute | solution.py:12
  111.0 41.9 %copy-start.10 = (bf16[128,256]{1,0:T(8,128)(2,1)S(1)}, bf16[128,256]{1,0:T(8,128)(2,1)}, u32[]{:S(2)}) copy-start(bf16[128,256]{1,0:T(8,128)(2,1)} %param.15) | copy-start | bytes 196612
  111.9 396.8 %all-reduce.3.cloned.1.call-start = ((), (), s32[]{:S(2)}) async-start(), calls=%async_computation.4 | async-start | bytes 1048576 | tf_op jit(solution)/shard_map/psum | solution.py:67
  112.0 42.7 %copy-start.12 = (f32[128]{0:T(128)}, f32[128]{0:T(128)S(1)}, u32[]{:S(2)}) copy-start(f32[128]{0:T(128)S(1)} %convert_sqrt_fusion) | copy-start | bytes 1540
  174.5 11.4 %collective-permute-start.8 = (bf16[512,256]{1,0:T(8,128)(2,1)S(1)}, bf16[512,256]{1,0:T(8,128)(2,1)S(1)}, u32[]{:S(2)}, u32[]{:S(2)}) collective-permute-start(bf16[512,256]{1,0:T(8,128)(2,1)S(1)} %bitcast.78), channel_id=1, source_target_pairs={{0,252},{4,0},{8,4},{12,8},{16,12},{20,16},{24,20},{28,24},{32,28}... | collective-permute-start | bytes 786440 | tf_op jit(solution)/shard_map/ppermute | solution.py:12
  186.0 10.5 %collective-permute-start.9 = (bf16[512,256]{1,0:T(8,128)(2,1)S(1)}, bf16[512,256]{1,0:T(8,128)(2,1)S(1)}, u32[]{:S(2)}, u32[]{:S(2)}) collective-permute-start(bf16[512,256]{1,0:T(8,128)(2,1)S(1)} %fusion.11), channel_id=1, source_target_pairs={{0,252},{4,0},{8,4},{12,8},{16,12},{20,16},{24,20},{28,24},{32,28}... | collective-permute-start | bytes 786440 | tf_op jit(solution)/shard_map/ppermute | solution.py:12
  196.5 10.3 %collective-permute-start.10 = (bf16[512,256]{1,0:T(8,128)(2,1)S(1)}, bf16[512,256]{1,0:T(8,128)(2,1)S(1)}, u32[]{:S(2)}, u32[]{:S(2)}) collective-permute-start(bf16[512,256]{1,0:T(8,128)(2,1)S(1)} %fusion.10), channel_id=1, source_target_pairs={{0,252},{4,0},{8,4},{12,8},{16,12},{20,16},{24,20},{28,24},{32,28}... | collective-permute-start | bytes 786440 | tf_op jit(solution)/shard_map/ppermute | solution.py:12
  206.9 9.8 %collective-permute-start.11 = (bf16[512,256]{1,0:T(8,128)(2,1)S(1)}, bf16[512,256]{1,0:T(8,128)(2,1)S(1)}, u32[]{:S(2)}, u32[]{:S(2)}) collective-permute-start(bf16[512,256]{1,0:T(8,128)(2,1)S(1)} %fusion.9), channel_id=1, source_target_pairs={{0,252},{4,0},{8,4},{12,8},{16,12},{20,16},{24,20},{28,24},{32,28}... | collective-permute-start | bytes 786440 | tf_op jit(solution)/shard_map/ppermute | solution.py:12
  216.7 25.4 %copy-start.9 = (f32[128,256]{1,0:T(8,128)S(1)}, f32[128,256]{1,0:T(8,128)}, u32[]{:S(2)}) copy-start(f32[128,256]{1,0:T(8,128)} %reduce-scatter.3.cloned.1.call-done) | copy-start | bytes 393220
  216.8 25.4 %copy-start.13 = (f32[128]{0:T(128)S(1)}, f32[128]{0:T(128)}, u32[]{:S(2)}) copy-start(f32[128]{0:T(128)} %copy-done.12) | copy-start | bytes 1540
  216.8 9.5 %collective-permute-start.12 = (bf16[512,256]{1,0:T(8,128)(2,1)S(1)}, bf16[512,256]{1,0:T(8,128)(2,1)S(1)}, u32[]{:S(2)}, u32[]{:S(2)}) collective-permute-start(bf16[512,256]{1,0:T(8,128)(2,1)S(1)} %fusion.8), channel_id=1, source_target_pairs={{0,252},{4,0},{8,4},{12,8},{16,12},{20,16},{24,20},{28,24},{32,28}... | collective-permute-start | bytes 786440 | tf_op jit(solution)/shard_map/ppermute | solution.py:12
  226.3 9.5 %collective-permute-start.13 = (bf16[512,256]{1,0:T(8,128)(2,1)S(1)}, bf16[512,256]{1,0:T(8,128)(2,1)S(1)}, u32[]{:S(2)}, u32[]{:S(2)}) collective-permute-start(bf16[512,256]{1,0:T(8,128)(2,1)S(1)} %fusion.7), channel_id=1, source_target_pairs={{0,252},{4,0},{8,4},{12,8},{16,12},{20,16},{24,20},{28,24},{32,28}... | collective-permute-start | bytes 786440 | tf_op jit(solution)/shard_map/ppermute | solution.py:12
  235.9 9.5 %collective-permute-start.14 = (bf16[512,256]{1,0:T(8,128)(2,1)S(1)}, bf16[512,256]{1,0:T(8,128)(2,1)S(1)}, u32[]{:S(2)}, u32[]{:S(2)}) collective-permute-start(bf16[512,256]{1,0:T(8,128)(2,1)S(1)} %fusion.6), channel_id=1, source_target_pairs={{0,252},{4,0},{8,4},{12,8},{16,12},{20,16},{24,20},{28,24},{32,28}... | collective-permute-start | bytes 786440 | tf_op jit(solution)/shard_map/ppermute | solution.py:12
  245.5 11.6 %collective-permute-start.15 = (bf16[512,256]{1,0:T(8,128)(2,1)S(1)}, bf16[512,256]{1,0:T(8,128)(2,1)S(1)}, u32[]{:S(2)}, u32[]{:S(2)}) collective-permute-start(bf16[512,256]{1,0:T(8,128)(2,1)S(1)} %fusion.5), channel_id=1, source_target_pairs={{0,12},{4,16},{8,20},{12,24},{16,28},{20,32},{24,36},{28,40},{32,4... | collective-permute-start | bytes 786440 | tf_op jit(solution)/shard_map/ppermute | solution.py:12
  246.5 297.1 %reduce-scatter.5.cloned.1.call-start = ((), (), s32[]{:S(2)}) async-start(), calls=%async_computation.3 | async-start | bytes 327680 | tf_op jit(solution)/shard_map/reduce_scatter | solution.py:97
  (9 other events, 43.3 us)
Sparse Core Ops, SparseCore 0:
  112.0 40.8 reduce-scatter.2
  246.7 261.9 all-reduce.2
  511.4 32.1 reduce-scatter.4
where the time goes:
time: 552 us
  waiting for transfers between devices  387 us (70%)
  starting transfers between devices  93.3 us (17%)
  other arithmetic  33.6 us (6%)
  between operations  14.1 us (3%)
  matrix products  12.5 us (2%)
  blocking collectives  8.14 us (1%)
    psum x1, waiting for transfers between devices, on_device(): lax.psum((local_self, local_neigh), ('blk', 'rep'))  251 us
    ppermute x16, starting transfers between devices, from_behind(): return lax.ppermute(value, axis, pairs)  93.2 us
    ppermute x16, waiting for transfers between devices, from_behind(): return lax.ppermute(value, axis, pairs)  63.5 us
    reduce_scatter x1, waiting for transfers between devices, on_device(): shared = lax.psum_scatter(summed, 'rep', scatter_dimension=0, tiled=True)  40.7 us
    reduce_scatter x1, waiting for transfers between devices, on_device(): lax.psum_scatter(carried.astype(jnp.bfloat16), 'rep', scatter_dimension=0...  31.6 us
    scatter-add x2, other arithmetic, backward_term(): placed = jnp.zeros((block_count, tile_size, feature_dim), jnp.float32).at...  11.7 us
    scatter-add x2, other arithmetic, forward_term(): placed = jnp.zeros((block_count, tile_size, feature_dim), jnp.float32).at...  11.7 us
  transfers between devices with their start and end apart: 19, of which 18 were waited for; matrix products, arithmetic and copies ran while one was open for 3% of the time, Pallas kernels for 0%

commit v1 on v0

v1 whole, which is shorter than its diff:
```python
import functools
import math

import jax
import jax.numpy as jnp
from jax import lax
from jax.experimental import pallas as pl
from jax.experimental.pallas import tpu as pltpu
from jax.sharding import PartitionSpec as P

Y, X_LO, Z, X_HI = 4, 2, 8, 2
X = X_LO * X_HI
MESH = pl.DeviceIdType.MESH
F32, BF16 = jnp.float32, jnp.bfloat16


def flag(cond):
    return jnp.where(cond, 1, 0)


def layer_kernel(
    tiles_hbm, coords, live, feat_hbm, degree, w_self, w_neigh, cot,
    hidden, grad_feat, grad_self, grad_neigh,
    tiles, own, panels, dense, dense_t, pair_out, pair_in, chip_out, chip_in, back,
    wpair_out, wpair_in, wy_out, wy_in, wx_out, wx_in, wz_all, wgrad,
    terms, chain_out, chain_in, final_in,
    local_sem, feat_send, relay_send, feat_recv, rep_send, rep_recv, back_send, back_recv,
    wpair_sem, wy_send, wy_recv, wx_send, wx_recv, wz_send, wz_recv, ax_send, ax_recv, ay_send, ay_recv, ac_sem,
    chain_send, chain_recv, final_recv,
):
    blk_total = Y * X_LO * Z
    b, r = lax.axis_index("blk"), lax.axis_index("rep")
    z, x_lo, y = b % Z, (b // Z) % X_LO, b // (Z * X_LO)
    x_hi, core = r // 2, r % 2
    x = x_hi * X_LO + x_lo
    tile = tiles.shape[2]
    depth = own.shape[1]
    rows = panels.shape[1]
    blocks = rows // tile
    tile_count = tiles.shape[1]
    up = jnp.where(x_hi == 0, 1, blk_total - 1)
    b_up = (b + up) % blk_total
    b_down = (b + blk_total - up) % blk_total

    def y_peer(step):
        return (((y + step) % Y) * X_LO + x_lo) * Z + z, r

    def x_peer(step):
        at = (x + step) % X
        return (y * X_LO + at % X_LO) * Z + z, (at // X_LO) * 2 + core

    def z_peer(step):
        return (y * X_LO + x_lo) * Z + (z + step) % Z, r

    sibling = (b, r + 1 - 2 * core)
    across = (b, (r + 2) % 4)

    def remote(src, dst, send, recv, peer):
        return pltpu.make_async_remote_copy(
            src_ref=src, dst_ref=dst, send_sem=send, recv_sem=recv, device_id=peer, device_id_type=MESH
        )

    def arrived(dst, send, recv):
        remote(dst, dst, send, recv, sibling).wait_recv()

    def chunk(index, size=tile):
        return pl.ds(pl.multiple_of(index * size, size), size)

    tile_copy = pltpu.make_async_copy(tiles_hbm.at[0], tiles, local_sem.at[0])
    tile_copy.start()
    own_copy = pltpu.make_async_copy(feat_hbm.at[chunk(r)], own, local_sem.at[1])
    own_copy.start()

    panel_copy = pltpu.make_async_copy(feat_hbm, panels.at[0], local_sem.at[2])

    @pl.when(r == 2)
    def _():
        panel_copy.start()

    barrier = pltpu.get_barrier_semaphore()
    greeted = 0
    peers = [(b_next, (r + turn) % 4) for b_next in (b_up, b_down) for turn in range(4)]
    peers += [(b, (r + turn) % 4) for turn in range(1, 4)]
    peers += [y_peer(step) for step in range(1, Y)]
    peers += [x_peer(step) for step in range(1, X)]
    peers += [z_peer(step) for step in range(1, Z)]
    for peer in peers:
        pl.semaphore_signal(barrier, inc=1, device_id=peer, device_id_type=MESH)
        greeted += 1
    pl.semaphore_wait(barrier, greeted)

    first = (r == 1) | (r == 2)
    relay_slot = jnp.where(r == 3, 0, 1)
    relay_rep = jnp.where(r == 2, 3, r)

    def first_send(j):
        return remote(
            feat_hbm.at[chunk(j)], panels.at[1, chunk(j)], feat_send.at[j], feat_recv.at[1, j], (b_up, r)
        )

    def relay_a(j):
        return remote(
            panels.at[relay_slot, chunk(j)], panels.at[1 - relay_slot, chunk(j)],
            relay_send.at[0, j], feat_recv.at[1 - relay_slot, j], (b_up, relay_rep),
        )

    def relay_b(j):
        return remote(
            panels.at[0, chunk(j)], panels.at[1, chunk(j)], relay_send.at[1, j], feat_recv.at[1, j], (b_up, 0)
        )

    def panel_arrived(slot, j):
        arrived(panels.at[slot, chunk(j)], feat_send.at[j], feat_recv.at[slot, j])

    @pl.when(first)
    def _():
        @pl.loop(0, blocks)
        def _(j):
            first_send(j).start()

    tile_copy.wait()
    own_copy.wait()

    def build(slot, i):
        at = (i % 2) * 2 + i // 2

        @pl.loop(0, blocks)
        def _(j):
            total = jnp.zeros((tile, tile), F32)
            for k in range(tile_count):
                here = (coords[0, slot, k, 0] == i) & (coords[0, slot, k, 1] == j)
                weight = (flag(here) * live[0, slot, k]).astype(F32)
                total += tiles[slot, k].astype(F32) * weight
            dense[slot, chunk(at), chunk(j)] = total.astype(BF16)
            dense_t[slot, chunk(j), chunk(at)] = total.T.astype(BF16)

    @pl.loop(0, blocks)
    def _(j):
        build(0, j)
        panel_arrived(relay_slot, j)
        relay_a(j).start()

    @pl.loop(0, blocks)
    def _(j):
        build(1, j)

        @pl.when(r == 1)
        def _():
            panel_arrived(0, j)
            relay_b(j).start()

    own_rows = own[...]
    pre_self = jnp.dot(own_rows, w_self[...], preferred_element_type=F32)
    degrees = jnp.broadcast_to(degree[...].astype(F32), (tile, tile))
    root_half = jnp.sqrt(degrees.T)
    root = jnp.concatenate([root_half] * (depth // tile), axis=1)

    @pl.when(r == 2)
    def _():
        panel_copy.wait()

    @pl.when(r == 0)
    def _():
        @pl.loop(0, blocks)
        def _(j):
            panel_arrived(0, j)

    @pl.when((r == 2) | (r == 3))
    def _():
        @pl.when(r == 3)
        def _():
            @pl.loop(0, blocks)
            def _(j):
                panel_arrived(1, j)

    def products(first_row, count):
        wanted = pl.ds(pl.multiple_of(first_row, count), count)
        return jnp.dot(dense[0, wanted, :], panels[0], preferred_element_type=F32) + jnp.dot(
            dense[1, wanted, :], panels[1], preferred_element_type=F32
        )

    half = rows // 2
    pair_out[...] = products((1 - core) * half, half).astype(BF16)
    pair_copy = remote(pair_out, pair_in, rep_send.at[0], rep_recv.at[0], sibling)
    pair_copy.start()
    terms[0, pl.ds(0, half), :] = products(core * half, half)
    pair_copy.wait_recv()
    other_chip, this_chip = chunk(1 - x_hi), chunk(x_hi)
    chip_out[...] = (terms[0, other_chip, :] + pair_in[other_chip, :].astype(F32)).astype(BF16)
    chip_copy = remote(chip_out, chip_in, rep_send.at[1], rep_recv.at[1], across)
    chip_copy.start()
    partial = terms[0, this_chip, :] + pair_in[this_chip, :].astype(F32)
    chip_copy.wait_recv()
    aggregate = ((partial + chip_in[...].astype(F32)) / root).astype(BF16)

    preact = pre_self + jnp.dot(aggregate, w_neigh[...], preferred_element_type=F32)
    sigmoid_pre = jax.nn.sigmoid(preact)
    slope = sigmoid_pre * (1.0 + preact * (1.0 - sigmoid_pre))
    grad_pre = (cot[...].astype(F32) * slope).astype(BF16)
    last = (((1,), (1,)), ((), ()))
    back_proj = (lax.dot_general(grad_pre, w_neigh[...], last, preferred_element_type=F32) / root).astype(BF16)

    def place(rep):
        return chunk((rep % 2) * 2 + rep // 2)

    back[place(r), :] = back_proj
    to_across = remote(back.at[place(r)], back.at[place(r)], back_send.at[0], back_recv.at[0], across)
    to_across.start()
    to_sibling = remote(back.at[place(r)], back.at[place(r)], back_send.at[1], back_recv.at[1], sibling)
    to_sibling.start()

    outer = (((0,), (0,)), ((), ()))
    is_first_core = core == 0
    given = jnp.where(is_first_core, aggregate, own_rows)
    kept = jnp.where(is_first_core, own_rows, aggregate)
    wpair_out[...] = lax.dot_general(given, grad_pre, outer, preferred_element_type=F32).astype(BF16)
    wpair_copy = remote(wpair_out, wpair_in, wpair_sem.at[0], wpair_sem.at[1], sibling)
    wpair_copy.start()
    hidden[...] = (preact * sigmoid_pre).astype(BF16)
    weight_sum = lax.dot_general(kept, grad_pre, outer, preferred_element_type=F32)
    own_term = lax.dot_general(grad_pre, w_self[...], last, preferred_element_type=F32)

    wpair_copy.wait_recv()
    terms[1, pl.ds(0, depth), :] = weight_sum + wpair_in[...].astype(F32)
    wy_out[...] = terms[1, pl.ds(0, depth), :].astype(BF16)
    y_rows = depth // Y
    x_rows = y_rows // X

    def wy_copy(step):
        return remote(
            wy_out.at[chunk((y + step) % Y, y_rows)], wy_in.at[step - 1],
            wy_send.at[step - 1], wy_recv.at[step - 1], y_peer(step),
        )

    for step in range(1, Y):
        wy_copy(step).start()
    y_sum = terms[1, chunk(y, y_rows), :]

    to_across.wait_recv()
    passed = place((r + 2) % 4)
    passed_on = remote(back.at[passed], back.at[passed], back_send.at[2], back_recv.at[2], sibling)
    passed_on.start()
    to_sibling.wait_recv()
    passed_on.wait_recv()

    slot_a = jnp.where((r == 0) | (r == 2), 1, 0)
    slot_b = 1 - slot_a
    starts = (r == 0) | (r == 3)
    ends = (r == 1) | (r == 2)

    def compute_terms(slot):
        terms[slot] = jnp.dot(dense_t[slot], back[...], preferred_element_type=F32)

    def start_send(j):
        return remote(
            chain_out.at[slot_b, chunk(j)], chain_in.at[slot_a, chunk(j)],
            chain_send.at[slot_b, j], chain_recv.at[slot_a, j], (b_down, r),
        )

    def chain_send_a(j):
        return remote(
            chain_out.at[slot_a, chunk(j)], chain_in.at[slot_b, chunk(j)],
            chain_send.at[slot_a, j], chain_recv.at[slot_b, j], (b_down, 1 + x_hi),
        )

    def final_send_up(j):
        return remote(
            chain_out.at[slot_b, chunk(j)], final_in.at[0], chain_send.at[slot_b, j], final_recv.at[0], (b_down, j)
        )

    def final_send_here(j):
        return remote(
            chain_out.at[slot_b, chunk(j)], final_in.at[1], chain_send.at[slot_b, j], final_recv.at[1], (b, j)
        )

    def chain_arrived(slot, j):
        arrived(chain_in.at[slot, chunk(j)], chain_send.at[slot, j], chain_recv.at[slot, j])

    def summed_chunk(slot, j):
        chain_out[slot, chunk(j), :] = (
            terms[slot, chunk(j), :] + chain_in[slot, chunk(j), :].astype(F32)
        ).astype(BF16)

    compute_terms(slot_b)

    @pl.when(starts)
    def _():
        @pl.loop(0, blocks)
        def _(j):
            chain_out[slot_b, chunk(j), :] = terms[slot_b, chunk(j), :].astype(BF16)
            start_send(j).start()

    compute_terms(slot_a)

    def chain_step_a(j):
        chain_arrived(slot_a, j)
        summed_chunk(slot_a, j)
        chain_send_a(j).start()

    def chain_step_b(j):
        @pl.when(ends)
        def _():
            chain_arrived(slot_b, j)
            summed_chunk(slot_b, j)

        @pl.when(r == 1)
        def _():
            final_send_up(j).start()

        @pl.when((r == 2) & (j != 2))
        def _():
            final_send_here(j).start()

    for step in range(1, Y):
        arrived(wy_in.at[step - 1], wy_send.at[step - 1], wy_recv.at[step - 1])
        y_sum += wy_in[step - 1].astype(F32)
    wx_out[...] = y_sum.astype(BF16)

    def wx_copy(step):
        return remote(
            wx_out.at[chunk((x + step) % X, x_rows)], wx_in.at[step - 1],
            wx_send.at[step - 1], wx_recv.at[step - 1], x_peer(step),
        )

    for step in range(1, X):
        wx_copy(step).start()

    for j in range(0, 2):
        chain_step_a(j)

    x_sum = wx_out[chunk(x, x_rows), :].astype(F32)
    for step in range(1, X):
        arrived(wx_in.at[step - 1], wx_send.at[step - 1], wx_recv.at[step - 1])
        x_sum += wx_in[step - 1].astype(F32)
    wz_all[z] = x_sum.astype(BF16)

    def wz_copy(step):
        return remote(wz_all.at[z], wz_all.at[z], wz_send.at[step - 1], wz_recv.at[step - 1], z_peer(step))

    for step in range(1, Z):
        wz_copy(step).start()

    for j in range(2, blocks):
        chain_step_a(j)
    for j in range(0, 2):
        chain_step_b(j)

    for step in range(1, Z):
        source = (z + Z - step) % Z
        arrived(wz_all.at[source], wz_send.at[step - 1], wz_recv.at[step - 1])
    z_sum = wz_all[0].astype(F32)
    for index in range(1, Z):
        z_sum += wz_all[index].astype(F32)
    mine = chunk((core * Y + y) * X + x, x_rows)
    wgrad[mine, :] = z_sum.astype(BF16)

    def ax_copy(step):
        return remote(wgrad.at[mine], wgrad.at[mine], ax_send.at[step - 1], ax_recv.at[step - 1], x_peer(step))

    for step in range(1, X):
        ax_copy(step).start()

    for j in range(2, blocks):
        chain_step_b(j)

    for step in range(1, X):
        theirs = chunk((core * Y + y) * X + (x + X - step) % X, x_rows)
        arrived(wgrad.at[theirs], ax_send.at[step - 1], ax_recv.at[step - 1])
    my_y = chunk(core * Y + y, y_rows)

    def ay_copy(step):
        return remote(wgrad.at[my_y], wgrad.at[my_y], ay_send.at[step - 1], ay_recv.at[step - 1], y_peer(step))

    for step in range(1, Y):
        ay_copy(step).start()

    arrived(final_in.at[0], chain_send.at[0, 0], final_recv.at[0])

    @pl.when(r == 2)
    def _():
        final_in[1] = chain_out[0, chunk(2), :]

    @pl.when(r != 2)
    def _():
        arrived(final_in.at[1], chain_send.at[0, 0], final_recv.at[1])

    grad_feat[...] = (own_term + final_in[0].astype(F32) + final_in[1].astype(F32)).astype(BF16)

    for step in range(1, Y):
        theirs = chunk(core * Y + (y + Y - step) % Y, y_rows)
        arrived(wgrad.at[theirs], ay_send.at[step - 1], ay_recv.at[step - 1])
    my_half = chunk(core, depth)
    half_copy = remote(wgrad.at[my_half], wgrad.at[my_half], ac_sem.at[0], ac_sem.at[1], sibling)
    half_copy.start()

    @pl.when(first)
    def _():
        @pl.loop(0, blocks)
        def _(j):
            first_send(j).wait_send()

    @pl.loop(0, blocks)
    def _(j):
        relay_a(j).wait_send()
        chain_send_a(j).wait_send()

        @pl.when(r == 1)
        def _():
            relay_b(j).wait_send()
            final_send_up(j).wait_send()

        @pl.when((r == 2) & (j != 2))
        def _():
            final_send_here(j).wait_send()

        @pl.when(starts)
        def _():
            start_send(j).wait_send()

    pair_copy.wait_send()
    chip_copy.wait_send()
    to_across.wait_send()
    to_sibling.wait_send()
    passed_on.wait_send()
    wpair_copy.wait_send()
    for step in range(1, Y):
        wy_copy(step).wait_send()
        ay_copy(step).wait_send()
    for step in range(1, X):
        wx_copy(step).wait_send()
        ax_copy(step).wait_send()
    for step in range(1, Z):
        wz_copy(step).wait_send()

    scale = 1.0 / math.sqrt(rows * blk_total)
    arrived(wgrad.at[chunk(1 - core, depth)], ac_sem.at[0], ac_sem.at[1])
    grad_self[...] = wgrad[pl.ds(0, depth), :].astype(F32) * scale
    grad_neigh[...] = wgrad[pl.ds(depth, depth), :].astype(F32) * scale
    half_copy.wait_send()


def on_device(tile_vals, tile_coords, tile_live, features, degree, w_self, w_neigh, cotangent):
    tile_count, tile = tile_vals.shape[2:4]
    rows, depth = features.shape
    share = cotangent.shape[0]
    blocks = rows // tile
    half = rows // 2
    y_rows = depth // Y
    x_rows = y_rows // X
    any_space = pl.BlockSpec(memory_space=pl.ANY)
    smem = pl.BlockSpec(memory_space=pltpu.SMEM)
    vmem = pl.BlockSpec(memory_space=pltpu.VMEM)
    dma = pltpu.SemaphoreType.DMA
    return pl.pallas_call(
        layer_kernel,
        out_shape=(
            jax.ShapeDtypeStruct((share, depth), BF16),
            jax.ShapeDtypeStruct((share, depth), BF16),
            jax.ShapeDtypeStruct((depth, depth), F32),
            jax.ShapeDtypeStruct((depth, depth), F32),
        ),
        in_specs=[any_space, smem, smem, any_space, vmem, vmem, vmem, vmem],
        out_specs=(vmem, vmem, vmem, vmem),
        scratch_shapes=[
            pltpu.VMEM((2, tile_count, tile, tile), BF16),
            pltpu.VMEM((share, depth), BF16),
            pltpu.VMEM((2, rows, depth), BF16),
            pltpu.VMEM((2, rows, rows), BF16),
            pltpu.VMEM((2, rows, rows), BF16),
            pltpu.VMEM((half, depth), BF16),
            pltpu.VMEM((half, depth), BF16),
            pltpu.VMEM((share, depth), BF16),
            pltpu.VMEM((share, depth), BF16),
            pltpu.VMEM((rows, depth), BF16),
            pltpu.VMEM((depth, depth), BF16),
            pltpu.VMEM((depth, depth), BF16),
            pltpu.VMEM((depth, depth), BF16),
            pltpu.VMEM((Y - 1, y_rows, depth), BF16),
            pltpu.VMEM((y_rows, depth), BF16),
            pltpu.VMEM((X - 1, x_rows, depth), BF16),
            pltpu.VMEM((Z, x_rows, depth), BF16),
            pltpu.VMEM((2 * depth, depth), BF16),
            pltpu.VMEM((2, rows, depth), F32),
            pltpu.VMEM((2, rows, depth), BF16),
            pltpu.VMEM((2, rows, depth), BF16),
            pltpu.VMEM((2, share, depth), BF16),
            dma((3,)),
            dma((blocks,)),
            dma((2, blocks)),
            dma((2, blocks)),
            dma((2,)),
            dma((2,)),
            dma((3,)),
            dma((3,)),
            dma((2,)),
            dma((Y - 1,)),
            dma((Y - 1,)),
            dma((X - 1,)),
            dma((X - 1,)),
            dma((Z - 1,)),
            dma((Z - 1,)),
            dma((X - 1,)),
            dma((X - 1,)),
            dma((Y - 1,)),
            dma((Y - 1,)),
            dma((2,)),
            dma((2, blocks)),
            dma((2, blocks)),
            dma((2,)),
        ],
        compiler_params=pltpu.CompilerParams(collective_id=0, has_side_effects=True),
    )(
        tile_vals, tile_coords, tile_live, features,
        degree.reshape(1, share), w_self, w_neigh, cotangent,
    )


def solution(mesh):
    return jax.shard_map(
        on_device,
        mesh=mesh,
        in_specs=(
            P("blk", "rep", None, None, None),
            P("blk", "rep", None, None),
            P("blk", "rep", None),
            P("blk", None),
            P(("blk", "rep")),
            P(),
            P(),
            P(("blk", "rep"), None),
        ),
        out_specs=(P(("blk", "rep"), None), P(("blk", "rep"), None), P(), P()),
        check_vma=False,
    )
```

time: 552 us -> 70.1 us (0.13)
  waiting for transfers between devices: 387 us -> 0 us
  starting transfers between devices: 93.3 us -> 0 us
  Pallas kernels: 0 us -> 61.5 us
  other arithmetic: 33.6 us -> 0 us
  between operations: 14.1 us -> 0.64 us
  matrix products: 12.5 us -> 0 us
  blocking collectives: 8.14 us -> 0 us
    psum x1 -> x0, waiting for transfers between devices: 251 us -> none  [on_device(): lax.psum((local_self, local_neigh), ('blk', 'rep'))]
    ppermute x16 -> x0, starting transfers between devices: 93.2 us -> none  [from_behind(): return lax.ppermute(value, axis, pairs)]
    reduce_scatter x2 -> x0, waiting for transfers between devices: 72.3 us -> none  [the longest x1 40.7 us: on_device(): shared = lax.psum_scatter(summed, 'rep', scatter_dimension=0, tiled=True)]
    ppermute x16 -> x0, waiting for transfers between devices: 63.5 us -> none  [from_behind(): return lax.ppermute(value, axis, pairs)]
    pallas_call x0 -> x1, Pallas kernels: none -> 61.5 us  [on_device(): pl.pallas_call(layer_kernel, out_shape=(jax.ShapeDtypeStruct((share, dept...]
    scatter-add x4 -> x0, other arithmetic: 23.5 us -> none  [the longest x2 11.7 us: backward_term(): placed = jnp.zeros((block_count, tile_size, feature_dim), jnp.float32).at...]
    dot_general x10 -> x0, matrix products: 12.5 us -> none  [the longest x2 4.18 us: backward_term(): jnp.einsum('krc,krd->kcd', masked[slot_idx], sources, preferred_element_t...]
    all_gather x1 -> x0, blocking collectives: 8.14 us -> none  [on_device(): full_back = lax.all_gather(back_proj, 'rep', axis=0, tiled=True)]
  transfers between devices with their start and end apart: 19 -> 0, of which waited for: 18 -> 0; matrix products, arithmetic and copies ran while one was open for 3% -> 0% of each run, Pallas kernels for 0% -> 0%
where the time goes in v1:
time: 70.1 us; the launch traced here: 69.8 us
  Pallas kernels  61.5 us (88%)
  local copies, waits for them, and re-layouts  7.66 us (11%)
    pallas_call x1, Pallas kernels, on_device(): pl.pallas_call(layer_kernel, out_shape=(jax.ShapeDtypeStruct((share, dept...  61.5 us
    unnamed x5, local copies, waits for them, and re-layouts  7.66 us

profile of v1, /device:TPU:1, one launch (start us, length us, event | category | flops | bytes accessed | tf_op | source)
XLA Modules:
  0.0 69.8 jit_solution(7543971227855405449)
XLA Ops:
  0.6 1.4 %copy.12.coords = s32[1,2,20,2]{3,2,1,0:T(8,128)} copy(s32[1,2,20,2]{2,3,1,0:T(2,128)} %param.9) | data formatting | bytes 640 | tf_op args[1]
  2.0 61.5 %shard_map.111 = (bf16[128,256]{1,0:T(8,128)(2,1)}, bf16[128,256]{1,0:T(8,128)(2,1)}, f32[256,256]{1,0:T(8,128)}, f32[256,256]{1,0:T(8,128)}) custom-call(bf16[1,2,20,128,128]{4,3,2,1,0:T(8,128)(2,1)} %tiles_hbm.1, s32[1,2,20,2]{3,2,1,0:T(8,128)} %copy.12.coords, s32[1,2,20]{2,1,0:T(2,128)} %live.1, bf16[512,256]{1,0:T(8,128)(2,1)} %feat_hbm.1, ...), custom_call_target="tpu_custom_call" | custom-call | tf_op jit(solution)/shard_map/pallas_call | solution.py:454
  63.5 1.5 %copy.17 = bf16[128,256]{1,0:T(8,128)(2,1)} copy(bf16[128,256]{1,0:T(8,128)(2,1)} %get-tuple-element.8) | data formatting | bytes 131072
  65.0 1.5 %copy.18 = bf16[128,256]{1,0:T(8,128)(2,1)} copy(bf16[128,256]{1,0:T(8,128)(2,1)} %get-tuple-element.9) | data formatting | bytes 131072
  66.5 1.7 %copy.19 = f32[256,256]{1,0:T(8,128)} copy(f32[256,256]{1,0:T(8,128)} %get-tuple-element.10) | data formatting | bytes 524288
  68.1 1.7 %copy.20 = f32[256,256]{1,0:T(8,128)} copy(f32[256,256]{1,0:T(8,128)} %get-tuple-element.11) | data formatting | bytes 524288

commit v2 on v1

--- a/solution.py
+++ b/solution.py
@@ -1,3 +1,4 @@
+import functools
 import functools
 import math
 
@@ -10,6 +11,7 @@
 
 Y, X_LO, Z, X_HI = 4, 2, 8, 2
 X = X_LO * X_HI
+PLANE = X * Y
 MESH = pl.DeviceIdType.MESH
 F32, BF16 = jnp.float32, jnp.bfloat16
 
@@ -19,13 +21,14 @@
 
 
 def layer_kernel(
-    tiles_hbm, coords, live, feat_hbm, degree, w_self, w_neigh, cot,
-    hidden, grad_feat, grad_self, grad_neigh,
+    tiles_hbm, coords_hbm, live_hbm, feat_hbm, degree_hbm, w_self_hbm, w_neigh_hbm, cot_hbm,
+    hidden, grad_feat, wgrad,
+    coords, live, degree, w_self, w_neigh, cot,
     tiles, own, panels, dense, dense_t, pair_out, pair_in, chip_out, chip_in, back,
-    wpair_out, wpair_in, wy_out, wy_in, wx_out, wx_in, wz_all, wgrad,
+    wpair_out, wpair_in, plane_out, plane_in, z_all,
     terms, chain_out, chain_in, final_in,
     local_sem, feat_send, relay_send, feat_recv, rep_send, rep_recv, back_send, back_recv,
-    wpair_sem, wy_send, wy_recv, wx_send, wx_recv, wz_send, wz_recv, ax_send, ax_recv, ay_send, ay_recv, ac_sem,
+    wpair_sem, plane_send, plane_recv, z_send, z_recv, share_send, share_recv, half_sem,
     chain_send, chain_recv, final_recv,
 ):
     blk_total = Y * X_LO * Z
@@ -42,12 +45,15 @@
     b_up = (b + up) % blk_total
     b_down = (b + blk_total - up) % blk_total
 
-    def y_peer(step):
-        return (((y + step) % Y) * X_LO + x_lo) * Z + z, r
-
-    def x_peer(step):
-        at = (x + step) % X
-        return (y * X_LO + at % X_LO) * Z + z, (at // X_LO) * 2 + core
+    def plane_place(step):
+        return ((y + step // X) % Y) * X + (x + step) % X
+
+    def plane_source(step):
+        return ((y + Y - step // X) % Y) * X + (x + X - step % X) % X
+
+    def plane_peer(step):
+        at_x = (x + step) % X
+        return (((y + step // X) % Y) * X_LO + at_x % X_LO) * Z + z, (at_x // X_LO) * 2 + core
 
     def z_peer(step):
         return (y * X_LO + x_lo) * Z + (z + step) % Z, r
@@ -66,27 +72,32 @@
     def chunk(index, size=tile):
         return pl.ds(pl.multiple_of(index * size, size), size)
 
-    tile_copy = pltpu.make_async_copy(tiles_hbm.at[0], tiles, local_sem.at[0])
-    tile_copy.start()
-    own_copy = pltpu.make_async_copy(feat_hbm.at[chunk(r)], own, local_sem.at[1])
-    own_copy.start()
-
-    panel_copy = pltpu.make_async_copy(feat_hbm, panels.at[0], local_sem.at[2])
-
-    @pl.when(r == 2)
-    def _():
-        panel_copy.start()
+    staged = [
+        (coords_hbm, coords), (live_hbm, live), (tiles_hbm.at[0], tiles), (feat_hbm.at[chunk(r)], own),
+        (degree_hbm, degree), (w_self_hbm, w_self), (w_neigh_hbm, w_neigh), (cot_hbm, cot),
+    ]
+    staging = [
+        pltpu.make_async_copy(src, dst, local_sem.at[index + 1]) for index, (src, dst) in enumerate(staged)
+    ]
+
+    panel_copy = pltpu.make_async_copy(feat_hbm, panels.at[0], local_sem.at[0])
 
     barrier = pltpu.get_barrier_semaphore()
     greeted = 0
     peers = [(b_next, (r + turn) % 4) for b_next in (b_up, b_down) for turn in range(4)]
     peers += [(b, (r + turn) % 4) for turn in range(1, 4)]
-    peers += [y_peer(step) for step in range(1, Y)]
-    peers += [x_peer(step) for step in range(1, X)]
+    peers += [plane_peer(step) for step in range(1, PLANE)]
     peers += [z_peer(step) for step in range(1, Z)]
     for peer in peers:
         pl.semaphore_signal(barrier, inc=1, device_id=peer, device_id_type=MESH)
         greeted += 1
+    for copy in staging:
+        copy.start()
+
+    @pl.when(r == 2)
+    def _():
+        panel_copy.start()
+
     pl.semaphore_wait(barrier, greeted)
 
     first = (r == 1) | (r == 2)
@@ -118,8 +129,8 @@
         def _(j):
             first_send(j).start()
 
-    tile_copy.wait()
-    own_copy.wait()
+    for copy in staging:
+        copy.wait()
 
     def build(slot, i):
         at = (i % 2) * 2 + i // 2
@@ -128,7 +139,7 @@
         def _(j):
             total = jnp.zeros((tile, tile), F32)
             for k in range(tile_count):
-                here = (coords[0, slot, k, 0] == i) & (coords[0, slot, k, 1] == j)
+                here = (coords[0, slot, 0, k] == i) & (coords[0, slot, 1, k] == j)
                 weight = (flag(here) * live[0, slot, k]).astype(F32)
                 total += tiles[slot, k].astype(F32) * weight
             dense[slot, chunk(at), chunk(j)] = total.astype(BF16)
@@ -172,6 +183,21 @@
             @pl.loop(0, blocks)
             def _(j):
                 panel_arrived(1, j)
+
+    def panels_left():
+        @pl.when(first)
+        def _():
+            @pl.loop(0, blocks)
+            def _(j):
+                first_send(j).wait_send()
+
+        @pl.loop(0, blocks)
+        def _(j):
+            relay_a(j).wait_send()
+
+            @pl.when(r == 1)
+            def _():
+                relay_b(j).wait_send()
 
     def products(first_row, count):
         wanted = pl.ds(pl.multiple_of(first_row, count), count)
@@ -193,6 +219,10 @@
     chip_copy.wait_recv()
     aggregate = ((partial + chip_in[...].astype(F32)) / root).astype(BF16)
 
+    def sums_left():
+        pair_copy.wait_send()
+        chip_copy.wait_send()
+
     preact = pre_self + jnp.dot(aggregate, w_neigh[...], preferred_element_type=F32)
     sigmoid_pre = jax.nn.sigmoid(preact)
     slope = sigmoid_pre * (1.0 + preact * (1.0 - sigmoid_pre))
@@ -222,19 +252,21 @@
 
     wpair_copy.wait_recv()
     terms[1, pl.ds(0, depth), :] = weight_sum + wpair_in[...].astype(F32)
-    wy_out[...] = terms[1, pl.ds(0, depth), :].astype(BF16)
-    y_rows = depth // Y
-    x_rows = y_rows // X
-
-    def wy_copy(step):
-        return remote(
-            wy_out.at[chunk((y + step) % Y, y_rows)], wy_in.at[step - 1],
-            wy_send.at[step - 1], wy_recv.at[step - 1], y_peer(step),
-        )
-
-    for step in range(1, Y):
-        wy_copy(step).start()
-    y_sum = terms[1, chunk(y, y_rows), :]
+    plane_out[...] = terms[1, pl.ds(0, depth), :].astype(BF16)
+    share_rows = depth // PLANE
+
+    def plane_copy(step):
+        return remote(
+            plane_out.at[chunk(plane_place(step), share_rows)], plane_in.at[step - 1],
+            plane_send.at[step - 1], plane_recv.at[step - 1], plane_peer(step),
+        )
+
+    @pl.loop(1, PLANE)
+    def _(step):
+        plane_copy(step).start()
+
+    place_here = y * X + x
+    plane_sum = terms[1, chunk(place_here, share_rows), :]
 
     to_across.wait_recv()
     passed = place((r + 2) % 4)
@@ -243,6 +275,11 @@
     to_sibling.wait_recv()
     passed_on.wait_recv()
 
+    def back_left():
+        to_across.wait_send()
+        to_sibling.wait_send()
+        passed_on.wait_send()
+
     slot_a = jnp.where((r == 0) | (r == 2), 1, 0)
     slot_b = 1 - slot_a
     starts = (r == 0) | (r == 3)
@@ -311,132 +348,117 @@
         def _():
             final_send_here(j).start()
 
-    for step in range(1, Y):
-        arrived(wy_in.at[step - 1], wy_send.at[step - 1], wy_recv.at[step - 1])
-        y_sum += wy_in[step - 1].astype(F32)
-    wx_out[...] = y_sum.astype(BF16)
-
-    def wx_copy(step):
-        return remote(
-            wx_out.at[chunk((x + step) % X, x_rows)], wx_in.at[step - 1],
-            wx_send.at[step - 1], wx_recv.at[step - 1], x_peer(step),
-        )
-
-    for step in range(1, X):
-        wx_copy(step).start()
-
-    for j in range(0, 2):
-        chain_step_a(j)
-
-    x_sum = wx_out[chunk(x, x_rows), :].astype(F32)
-    for step in range(1, X):
-        arrived(wx_in.at[step - 1], wx_send.at[step - 1], wx_recv.at[step - 1])
-        x_sum += wx_in[step - 1].astype(F32)
-    wz_all[z] = x_sum.astype(BF16)
-
-    def wz_copy(step):
-        return remote(wz_all.at[z], wz_all.at[z], wz_send.at[step - 1], wz_recv.at[step - 1], z_peer(step))
+    def chain_left():
+        @pl.loop(0, blocks)
+        def _(j):
+            chain_send_a(j).wait_send()
+
+            @pl.when(r == 1)
+            def _():
+                final_send_up(j).wait_send()
+
+            @pl.when((r == 2) & (j != 2))
+            def _():
+                final_send_here(j).wait_send()
+
+            @pl.when(starts)
+            def _():
+                start_send(j).wait_send()
+
+    for step in range(1, PLANE):
+        arrived(plane_in.at[step - 1], plane_send.at[step - 1], plane_recv.at[step - 1])
+        plane_sum += plane_in[step - 1].astype(F32)
+    z_all[z] = plane_sum.astype(BF16)
+
+    def z_copy(step):
+        return remote(z_all.at[z], z_all.at[z], z_send.at[step - 1], z_recv.at[step - 1], z_peer(step))
 
     for step in range(1, Z):
-        wz_copy(step).start()
-
-    for j in range(2, blocks):
-        chain_step_a(j)
-    for j in range(0, 2):
-        chain_step_b(j)
+        z_copy(step).start()
+
+    @pl.when(starts)
+    def _():
+        @pl.loop(0, blocks)
+        def _(j):
+            chain_step_a(j)
 
     for step in range(1, Z):
-        source = (z + Z - step) % Z
-        arrived(wz_all.at[source], wz_send.at[step - 1], wz_recv.at[step - 1])
-    z_sum = wz_all[0].astype(F32)
+        arrived(z_all.at[(z + Z - step) % Z], z_send.at[step - 1], z_recv.at[step - 1])
+    z_sum = z_all[0].astype(F32)
     for index in range(1, Z):
-        z_sum += wz_all[index].astype(F32)
-    mine = chunk((core * Y + y) * X + x, x_rows)
-    wgrad[mine, :] = z_sum.astype(BF16)
-
-    def ax_copy(step):
-        return remote(wgrad.at[mine], wgrad.at[mine], ax_send.at[step - 1], ax_recv.at[step - 1], x_peer(step))
-
-    for step in range(1, X):
-        ax_copy(step).start()
-
-    for j in range(2, blocks):
-        chain_step_b(j)
-
-    for step in range(1, X):
-        theirs = chunk((core * Y + y) * X + (x + X - step) % X, x_rows)
-        arrived(wgrad.at[theirs], ax_send.at[step - 1], ax_recv.at[step - 1])
-    my_y = chunk(core * Y + y, y_rows)
-
-    def ay_copy(step):
-        return remote(wgrad.at[my_y], wgrad.at[my_y], ay_send.at[step - 1], ay_recv.at[step - 1], y_peer(step))
-
-    for step in range(1, Y):
-        ay_copy(step).start()
-
-    arrived(final_in.at[0], chain_send.at[0, 0], final_recv.at[0])
-
-    @pl.when(r == 2)
-    def _():
-        final_in[1] = chain_out[0, chunk(2), :]
-
-    @pl.when(r != 2)
-    def _():
-        arrived(final_in.at[1], chain_send.at[0, 0], final_recv.at[1])
-
-    grad_feat[...] = (own_term + final_in[0].astype(F32) + final_in[1].astype(F32)).astype(BF16)
-
-    for step in range(1, Y):
-        theirs = chunk(core * Y + (y + Y - step) % Y, y_rows)
-        arrived(wgrad.at[theirs], ay_send.at[step - 1], ay_recv.at[step - 1])
-    my_half = chunk(core, depth)
-    half_copy = remote(wgrad.at[my_half], wgrad.at[my_half], ac_sem.at[0], ac_sem.at[1], sibling)
-    half_copy.start()
-
-    @pl.when(first)
-    def _():
-        @pl.loop(0, blocks)
-        def _(j):
-            first_send(j).wait_send()
+        z_sum += z_all[index].astype(F32)
+
+    def share_at(place):
+        return chunk(core * PLANE + place, share_rows)
+
+    wgrad[share_at(place_here), :] = z_sum.astype(BF16)
+
+    def share_copy(step):
+        mine = share_at(place_here)
+        return remote(
+            wgrad.at[mine], wgrad.at[mine], share_send.at[step - 1], share_recv.at[step - 1], plane_peer(step)
+        )
+
+    @pl.loop(1, PLANE)
+    def _(step):
+        share_copy(step).start()
+
+    @pl.when(ends)
+    def _():
+        @pl.loop(0, blocks)
+        def _(j):
+            chain_step_a(j)
 
     @pl.loop(0, blocks)
     def _(j):
-        relay_a(j).wait_send()
-        chain_send_a(j).wait_send()
-
-        @pl.when(r == 1)
-        def _():
-            relay_b(j).wait_send()
-            final_send_up(j).wait_send()
-
-        @pl.when((r == 2) & (j != 2))
-        def _():
-            final_send_here(j).wait_send()
-
-        @pl.when(starts)
-        def _():
-            start_send(j).wait_send()
-
-    pair_copy.wait_send()
-    chip_copy.wait_send()
-    to_across.wait_send()
-    to_sibling.wait_send()
-    passed_on.wait_send()
-    wpair_copy.wait_send()
-    for step in range(1, Y):
-        wy_copy(step).wait_send()
-        ay_copy(step).wait_send()
-    for step in range(1, X):
-        wx_copy(step).wait_send()
-        ax_copy(step).wait_send()
-    for step in range(1, Z):
-        wz_copy(step).wait_send()
-
-    scale = 1.0 / math.sqrt(rows * blk_total)
-    arrived(wgrad.at[chunk(1 - core, depth)], ac_sem.at[0], ac_sem.at[1])
+        chain_step_b(j)
+
+    arrived(final_in.at[0], chain_send.at[0, 0], final_recv.at[0])
+
+    @pl.when(r == 2)
+    def _():
+        final_in[1] = chain_out[0, chunk(2), :]
+
+    @pl.when(r != 2)
+    def _():
+        arrived(final_in.at[1], chain_send.at[0, 0], final_recv.at[1])
+
+    grad_feat[...] = (own_term + final_in[0].astype(F32) + final_in[1].astype(F32)).astype(BF16)
+
+    @pl.loop(1, PLANE)
+    def _(step):
+        arrived(wgrad.at[share_at(plane_source(step))], share_send.at[step - 1], share_recv.at[step - 1])
+
+    my_half = chunk(core, depth)
+    half_copy = remote(wgrad.at[my_half], wgrad.at[my_half], half_sem.at[0], half_sem.at[1], sibling)
+    half_copy.start()
+
+    def weights_left():
+        wpair_copy.wait_send()
+
+        @pl.loop(1, PLANE)
+        def _(step):
+            plane_copy(step).wait_send()
+            share_copy(step).wait_send()
+
+        for step in range(1, Z):
+            z_copy(step).wait_send()
+
+    panels_left()
+    sums_left()
+    back_left()
+    chain_left()
+    weights_left()
+    arrived(wgrad.at[chunk(1 - core, depth)], half_sem.at[0], half_sem.at[1])
+    half_copy.wait_send()
+
+
+def result_kernel(hidden, grad_feat, wgrad, hidden_out, grad_feat_out, grad_self, grad_neigh, *, scale):
+    hidden_out[...] = hidden[...]
+    grad_feat_out[...] = grad_feat[...]
+    depth = grad_self.shape[0]
     grad_self[...] = wgrad[pl.ds(0, depth), :].astype(F32) * scale
     grad_neigh[...] = wgrad[pl.ds(depth, depth), :].astype(F32) * scale
-    half_copy.wait_send()
 
 
 def on_device(tile_vals, tile_coords, tile_live, features, degree, w_self, w_neigh, cotangent):
@@ -445,23 +467,24 @@
     share = cotangent.shape[0]
     blocks = rows // tile
     half = rows // 2
-    y_rows = depth // Y
-    x_rows = y_rows // X
+    share_rows = depth // PLANE
     any_space = pl.BlockSpec(memory_space=pl.ANY)
-    smem = pl.BlockSpec(memory_space=pltpu.SMEM)
     vmem = pl.BlockSpec(memory_space=pltpu.VMEM)
     dma = pltpu.SemaphoreType.DMA
-    return pl.pallas_call(
+    nodes = jax.ShapeDtypeStruct((share, depth), BF16)
+    weights = jax.ShapeDtypeStruct((depth, depth), F32)
+    hidden, grad_feat, wgrad = pl.pallas_call(
         layer_kernel,
-        out_shape=(
-            jax.ShapeDtypeStruct((share, depth), BF16),
-            jax.ShapeDtypeStruct((share, depth), BF16),
-            jax.ShapeDtypeStruct((depth, depth), F32),
-            jax.ShapeDtypeStruct((depth, depth), F32),
-        ),
-        in_specs=[any_space, smem, smem, any_space, vmem, vmem, vmem, vmem],
-        out_specs=(vmem, vmem, vmem, vmem),
+        out_shape=(nodes, nodes, jax.ShapeDtypeStruct((2 * depth, depth), BF16)),
+        in_specs=[any_space] * 8,
+        out_specs=(vmem, vmem, vmem),
         scratch_shapes=[
+            pltpu.SMEM((1, 2, 2, tile_count), jnp.int32),
+            pltpu.SMEM((1, 2, tile_count), jnp.int32),
+            pltpu.VMEM((1, share), jnp.int32),
+            pltpu.VMEM((depth, depth), BF16),
+            pltpu.VMEM((depth, depth), BF16),
+            pltpu.VMEM((share, depth), BF16),
             pltpu.VMEM((2, tile_count, tile, tile), BF16),
             pltpu.VMEM((share, depth), BF16),
             pltpu.VMEM((2, rows, depth), BF16),
@@ -475,16 +498,13 @@
             pltpu.VMEM((depth, depth), BF16),
             pltpu.VMEM((depth, depth), BF16),
             pltpu.VMEM((depth, depth), BF16),
-            pltpu.VMEM((Y - 1, y_rows, depth), BF16),
-            pltpu.VMEM((y_rows, depth), BF16),
-            pltpu.VMEM((X - 1, x_rows, depth), BF16),
-            pltpu.VMEM((Z, x_rows, depth), BF16),
-            pltpu.VMEM((2 * depth, depth), BF16),
+            pltpu.VMEM((PLANE - 1, share_rows, depth), BF16),
+            pltpu.VMEM((Z, share_rows, depth), BF16),
             pltpu.VMEM((2, rows, depth), F32),
             pltpu.VMEM((2, rows, depth), BF16),
             pltpu.VMEM((2, rows, depth), BF16),
             pltpu.VMEM((2, share, depth), BF16),
-            dma((3,)),
+            dma((9,)),
             dma((blocks,)),
             dma((2, blocks)),
             dma((2, blocks)),
@@ -493,16 +513,12 @@
             dma((3,)),
             dma((3,)),
             dma((2,)),
-            dma((Y - 1,)),
-            dma((Y - 1,)),
-            dma((X - 1,)),
-            dma((X - 1,)),
+            dma((PLANE - 1,)),
+            dma((PLANE - 1,)),
             dma((Z - 1,)),
             dma((Z - 1,)),
-            dma((X - 1,)),
-            dma((X - 1,)),
-            dma((Y - 1,)),
-            dma((Y - 1,)),
+            dma((PLANE - 1,)),
+            dma((PLANE - 1,)),
             dma((2,)),
             dma((2, blocks)),
             dma((2, blocks)),
@@ -510,9 +526,16 @@
         ],
         compiler_params=pltpu.CompilerParams(collective_id=0, has_side_effects=True),
     )(
-        tile_vals, tile_coords, tile_live, features,
+        tile_vals, jnp.swapaxes(tile_coords, 2, 3), tile_live, features,
         degree.reshape(1, share), w_self, w_neigh, cotangent,
     )
+    scale = 1.0 / math.sqrt(rows * lax.axis_size("blk"))
+    return pl.pallas_call(
+        functools.partial(result_kernel, scale=scale),
+        out_shape=(nodes, nodes, weights, weights),
+        in_specs=[vmem, vmem, vmem],
+        out_specs=(vmem, vmem, vmem, vmem),
+    )(hidden, grad_feat, wgrad)
 
 
 def solution(mesh):

time: 70.1 us -> 61.4 us (0.88)
  local copies, waits for them, and re-layouts: 7.66 us -> 0 us
  Pallas kernels: 61.5 us -> 60.7 us
    unnamed x5 -> x0, local copies, waits for them, and re-layouts: 7.66 us -> none
    pallas_call x1 -> x2, Pallas kernels: 61.5 us -> 60.7 us  [the longest x1 58.8 us: on_device(): pl.pallas_call(layer_kernel, out_shape=(nodes, nodes, jax.ShapeDtypeStruc...]
where the time goes in v2:
time: 61.4 us; the launch traced here: 61.3 us
  Pallas kernels  60.7 us (99%)
  between operations  0.64 us (1%)
    pallas_call x1, Pallas kernels, on_device(): pl.pallas_call(layer_kernel, out_shape=(nodes, nodes, jax.ShapeDtypeStruc...  58.8 us
    pallas_call x1, Pallas kernels, on_device(): pl.pallas_call(functools.partial(result_kernel, scale=scale), out_shape=(...  1.87 us

profile of v2, /device:TPU:1, one launch (start us, length us, event | category | flops | bytes accessed | tf_op | source)
XLA Modules:
  0.0 61.3 jit_solution(3119856286202352975)
XLA Ops:
  0.6 58.8 %shard_map.111 = (bf16[128,256]{1,0:T(8,128)(2,1)}, bf16[128,256]{1,0:T(8,128)(2,1)}, bf16[512,256]{1,0:T(8,128)(2,1)}) custom-call(bf16[1,2,20,128,128]{4,3,2,1,0:T(8,128)(2,1)} %tiles_hbm.1, s32[1,2,2,20]{3,2,1,0:T(2,128)} %bitcast.2, s32[1,2,20]{2,1,0:T(2,128)} %live_hbm.1, bf16[512,256]{1,0:T(8,128)(2,1)} %feat_hbm.1, s32[1,128]{1,0:T(1,128)} %bitcast.3, ...), custom_call_target="tpu_custom_call" | custom-call | tf_op jit(solution)/shard_map/pallas_call | solution.py:476
  59.4 1.9 %shard_map.112 = (bf16[128,256]{1,0:T(8,128)(2,1)}, bf16[128,256]{1,0:T(8,128)(2,1)}, f32[256,256]{1,0:T(8,128)}, f32[256,256]{1,0:T(8,128)}) custom-call(bf16[128,256]{1,0:T(8,128)(2,1)} %get-tuple-element.7.hidden, bf16[128,256]{1,0:T(8,128)(2,1)} %get-tuple-element.8.grad_feat, bf16[512,256]{1,0:T(8,128)(2,1)} %get-tuple-element.9.wgrad), custom_call_target="tpu_custom_call" | custom-call | tf_op jit(solution)/shard_map/pallas_call | solution.py:533
